TPU v7x, 32 devices: a whole 2x2x4 slice. The times are simulated.
32 devices in a mesh: gx: 4 (over y, core), gy: 8 (over z, x).
Axes of the slice: x: 2, y: 2, z: 4, core: 2. Of those that a mesh axis runs over, the one named last changes fastest.
Arguments:
- tokens: bfloat16 [4, 256, 6144], P('gx', None, 'gy'), may hold values from -6 to 6
- norm_gain: float32 [6144], replicated, may hold values from 0.1 to 1.9
- qkv_weight: bfloat16 [6144, 3, 4096], P('gx', None, 'gy'), may hold values from -0.078125 to 0.078125
- up_weight: bfloat16 [6144, 24576], P('gx', 'gy'), may hold values from -0.078125 to 0.078125
- query_gain: float32 [128], replicated, may hold values from 0.1 to 1.9
- key_gain: float32 [128], replicated, may hold values from 0.1 to 1.9
- out_weight: bfloat16 [4096, 6144], P('gy', 'gx'), may hold values from -0.09375 to 0.09375
- down_weight: bfloat16 [24576, 6144], P('gy', 'gx'), may hold values from -0.0390625 to 0.0390625
- attention_keep: int32 [4, 256, 6144], P('gx', None, 'gy'), may hold values 0 or 1
- feedforward_keep: int32 [4, 256, 6144], P('gx', None, 'gy'), may hold values 0 or 1
Outputs:
- block_out: bfloat16 [4, 256, 6144], P('gx', None, 'gy')
All inputs are finite; a program needn't handle non-finite values. No bound on the sum of `attention_keep` or of `feedforward_keep` on one device may be relied on, other than what follows from the above.
Results may differ from a plain program's by a relative error of at most 0.017.
Values may be sent and summed in bfloat16 or wider, within the bound.
A program may use at most 128 MiB of HBM per device.

v0:
```python
import jax
import jax.numpy as jnp
from jax import lax
from jax.sharding import PartitionSpec as P

epsilon = 1e-06
keep_scale = 1.0 / 0.9


def layer_norm(values, gain):
    center = values - jnp.mean(values, axis=-1, keepdims=True)
    variance = jnp.mean(center * center, axis=-1, keepdims=True)
    return center * lax.rsqrt(variance + epsilon) * gain


def head_norm(values, gain):
    row_count = values.shape[0]
    shaped = values.reshape(row_count, -1, gain.shape[0])
    return layer_norm(shaped, gain).reshape(row_count, -1)


def per_device(
    tokens,
    norm_gain,
    qkv_weight,
    up_weight,
    query_gain,
    key_gain,
    out_weight,
    down_weight,
    attention_keep,
    feedforward_keep,
):
    images, seq_len, slice_width = tokens.shape
    whole_rows = lax.all_gather(tokens, "gy", axis=2, tiled=True)
    model_width = whole_rows.shape[2]
    own_rows = images * seq_len
    normed = (
        layer_norm(whole_rows.astype(jnp.float32), norm_gain)
        .astype(jnp.bfloat16)
        .reshape(own_rows, model_width)
    )
    blocks = lax.all_to_all(normed, "gx", split_axis=1, concat_axis=0, tiled=True)
    block_width = blocks.shape[1]
    head_cols = qkv_weight.shape[2]
    head_size = query_gain.shape[0]
    qkv_flat = qkv_weight.reshape(block_width, 3 * head_cols)
    joined = jnp.concatenate([qkv_flat, up_weight], axis=1)
    united = lax.psum_scatter(
        jnp.dot(blocks, joined, preferred_element_type=jnp.float32).astype(jnp.bfloat16),
        "gx",
        scatter_dimension=0,
        tiled=True,
    ).astype(jnp.float32)
    queries = head_norm(united[:, :head_cols], query_gain).astype(jnp.bfloat16)
    keys = head_norm(united[:, head_cols : 2 * head_cols], key_gain).astype(jnp.bfloat16)
    values = united[:, 2 * head_cols : 3 * head_cols].astype(jnp.bfloat16)
    hidden = jax.nn.gelu(united[:, 3 * head_cols :], approximate=False).astype(jnp.bfloat16)
    query_grid = queries.reshape(images, seq_len, -1, head_size)
    key_grid = keys.reshape(images, seq_len, -1, head_size)
    value_grid = values.reshape(images, seq_len, -1, head_size)
    scores = jnp.einsum(
        "bshd,bthd->bhst", query_grid, key_grid, preferred_element_type=jnp.float32
    ) * head_size ** (-0.5)
    raised = jnp.exp(scores)
    weights = (raised / jnp.sum(raised, axis=-1, keepdims=True)).astype(jnp.bfloat16)
    attended = jnp.einsum(
        "bhst,bthd->bshd", weights, value_grid, preferred_element_type=jnp.float32
    )
    attended = attended.astype(jnp.bfloat16).reshape(own_rows, head_cols)
    attention_part = jnp.dot(
        lax.all_gather(attended, "gx", axis=0, tiled=True),
        out_weight,
        preferred_element_type=jnp.float32,
    )
    feedforward_part = jnp.dot(
        lax.all_gather(hidden, "gx", axis=0, tiled=True),
        down_weight,
        preferred_element_type=jnp.float32,
    )
    delivered = (
        lax.all_to_all(
            attention_part.astype(jnp.bfloat16), "gx", split_axis=0, concat_axis=1, tiled=True
        ),
        lax.all_to_all(
            feedforward_part.astype(jnp.bfloat16), "gx", split_axis=0, concat_axis=1, tiled=True
        ),
    )
    rounded = jnp.stack([delivered[0], delivered[1]])
    rounded = lax.optimization_barrier(rounded)
    totals = lax.psum_scatter(
        rounded.astype(jnp.float32).astype(jnp.bfloat16), "gy", scatter_dimension=2, tiled=True
    ).astype(jnp.float32)
    attention_out = totals[0].reshape(images, seq_len, slice_width)
    feedforward_out = totals[1].reshape(images, seq_len, slice_width)
    branches = (
        attention_keep.astype(jnp.float32) * attention_out
        + feedforward_keep.astype(jnp.float32) * feedforward_out
    )
    return (tokens.astype(jnp.float32) + branches * keep_scale).astype(jnp.bfloat16)


def solution(mesh):
    in_specs = (
        P("gx", None, "gy"),
        P(),
        P("gx", None, "gy"),
        P("gx", "gy"),
        P(),
        P(),
        P("gy", "gx"),
        P("gy", "gx"),
        P("gx", None, "gy"),
        P("gx", None, "gy"),
    )
    out_specs = P("gx", None, "gy")
    return jax.shard_map(
        per_device, mesh=mesh, in_specs=in_specs, out_specs=out_specs, check_vma=False
    )
```

profile of v0, /device:TPU:2, one launch (start us, length us, event | category | flops | bytes accessed | tf_op | source)
XLA Modules:
  0.0 533.0 jit_solution(1531559722905003716)
XLA Ops:
  8.6 61.3 %all-gather.4.cloned.1.call-done = bf16[1,256,6144]{1,2,0:T(8,128)(2,1)} async-done(((bf16[1,256,768]{1,2,0:T(8,128)(2,1)}), bf16[1,256,6144]{1,2,0:T(8,128)(2,1)}) %all-gather.4.cloned.1.call-update) | async-done | bytes 3145744 | tf_op jit(solution)/shard_map/all_gather | solution.py:35
  69.9 2.9 convert_reduce_fusion
  73.7 2.3 fusion.11
  75.9 4.7 all-to-all-start
  80.6 6.6 %copy.28 = bf16[1536,3,512]{0,2,1:T(8,128)(2,1)} copy(bf16[1536,3,512]{2,0,1:T(8,128)(2,1)} %param.12) | data formatting | bytes 9437184 | tf_op args[2]
  87.3 6.6 %copy.29 = bf16[1536,1536]{1,0:T(8,128)(2,1)} copy(bf16[1536,1536]{0,1:T(8,128)(2,1)} %bitcast.67) | data formatting | bytes 9437184 | tf_op jit(solution)/shard_map/reshape | solution.py:47
  93.9 23.7 %all-to-all-done = bf16[256,4,1536]{0,2,1:T(8,128)(2,1)} async-done(((bf16[256,4,1536]{0,2,1:T(8,128)(2,1)}), bf16[256,4,1536]{0,2,1:T(8,128)(2,1)}, u32[]{:S(2)}, u32[]{:S(2)}) %all-to-all-start) | async-done | bytes 3145760 | tf_op jit(solution)/shard_map/all_to_all | solution.py:43
  117.6 4.7 copy.27
  122.2 22.6 %fusion.4 = bf16[1024,4608]{1,0:T(8,128)(2,1)} fusion(bf16[1024,1536]{1,0:T(8,128)(2,1)} %bitcast.71, bf16[1536,3072]{1,0:T(8,128)(2,1)} %param.13, bf16[1536,1536]{1,0:T(8,128)(2,1)} %copy.29), kind=kOutput, calls=%fused_computation.4 | convolution fusion | flops 14528544768 | bytes 26738688 | tf_op jit(solution)/shard_map/dot_general | solution.py:50
  145.6 76.1 %reduce-scatter.3.cloned.1.call-done = bf16[256,4608]{1,0:T(8,128)(2,1)} async-done(((bf16[1024,4608]{1,0:T(8,128)(2,1)}), bf16[256,4608]{1,0:T(8,128)(2,1)}) %reduce-scatter.3.cloned.1.call-update) | async-done | bytes 2359312 | tf_op jit(solution)/shard_map/reduce_scatter | solution.py:49
  231.2 8.6 %fusion.14 = bf16[256,3072]{1,0:T(8,128)(2,1)} fusion(f32[256,4608]{1,0:T(8,128)} %copy-done.3), kind=kLoop, calls=%fused_computation.18 | loop fusion | flops 51118080 | bytes 4718592 | tf_op jit(solution)/shard_map/convert_element_type | solution.py:58
  239.8 8.3 %all-gather.6.cloned.1.call-done = bf16[1024,512]{0,1:T(8,128)(2,1)} async-done(((bf16[256,512]{0,1:T(8,128)(2,1)}), bf16[1024,512]{0,1:T(8,128)(2,1)}) %all-gather.6.cloned.1.call-update) | async-done | bytes 1048592 | tf_op jit(solution)/shard_map/all_gather | solution.py:72
  248.1 4.7 convolution_convert_fusion.1
  252.8 4.7 all-to-all-start.1
  257.6 72.0 %all-gather.8.cloned.1.call-done = bf16[1024,3072]{1,0:T(8,128)(2,1)} async-done(((bf16[256,3072]{1,0:T(8,128)(2,1)}), bf16[1024,3072]{1,0:T(8,128)(2,1)}) %all-gather.8.cloned.1.call-update) | async-done | bytes 6291472 | tf_op jit(solution)/shard_map/all_gather | solution.py:77
  329.6 15.6 %convolution_convert_fusion = bf16[1024,1536]{1,0:T(8,128)(2,1)} fusion(bf16[1024,3072]{1,0:T(8,128)(2,1)} %all-gather.8.cloned.1.call-done, bf16[3072,1536]{1,0:T(8,128)(2,1)} %param.17), kind=kOutput, calls=%fused_computation.14 | convolution fusion | flops 9665249280 | bytes 18874368 | tf_op jit(solution)/shard_map/dot_general | solution.py:76
  345.2 4.9 all-to-all-start.2
  350.1 6.0 %copy.34 = bf16[256,4,1536]{2,1,0:T(4,128)(2,1)} copy(bf16[256,4,1536]{2,0,1:T(8,128)(2,1)} %bitcast.11) | data formatting | bytes 6291456 | tf_op jit(solution)/shard_map/all_to_all | solution.py:82
  356.1 6.9 %stack.9 = bf16[1,256,6144]{2,1,0:T(8,128)(2,1)} reshape(bf16[256,4,1536]{2,1,0:T(4,128)(2,1)} %copy.34) | data formatting | bytes 6291456 | tf_op jit(solution)/shard_map/stack | solution.py:89
  363.0 24.0 %all-to-all-done.2 = bf16[4,256,1536]{2,1,0:T(8,128)(2,1)} async-done(((bf16[4,256,1536]{2,1,0:T(8,128)(2,1)}), bf16[4,256,1536]{2,1,0:T(8,128)(2,1)}, u32[]{:S(2)}, u32[]{:S(2)}) %all-to-all-start.2) | async-done | bytes 3145760 | tf_op jit(solution)/shard_map/all_to_all | solution.py:85
  387.0 6.0 %copy.35 = bf16[256,4,1536]{2,1,0:T(4,128)(2,1)} copy(bf16[256,4,1536]{2,0,1:T(8,128)(2,1)} %bitcast.13) | data formatting | bytes 6291456 | tf_op jit(solution)/shard_map/all_to_all | solution.py:85
  393.0 6.9 %stack.10 = bf16[1,256,6144]{2,1,0:T(8,128)(2,1)} reshape(bf16[256,4,1536]{2,1,0:T(4,128)(2,1)} %copy.35) | data formatting | bytes 6291456 | tf_op jit(solution)/shard_map/stack | solution.py:89
  399.9 6.1 %pad_maximum_fusion = bf16[2,256,6144]{2,1,0:T(8,128)(2,1)} fusion(bf16[1,256,6144]{2,1,0:T(8,128)(2,1)} %stack.10, bf16[1,256,6144]{2,1,0:T(8,128)(2,1)} %stack.9), kind=kLoop, calls=%fused_computation.12 | loop fusion | flops 3145728 | bytes 12582912 | tf_op jit(solution)/shard_map/stack | solution.py:89
  406.0 118.1 %reduce-scatter.5.cloned.1.call-done = bf16[2,256,768]{2,1,0:T(8,128)(2,1)} async-done(((bf16[2,256,6144]{2,1,0:T(8,128)(2,1)}), bf16[2,256,768]{2,1,0:T(8,128)(2,1)}) %reduce-scatter.5.cloned.1.call-update) | async-done | bytes 786448 | tf_op jit(solution)/shard_map/reduce_scatter | solution.py:91
  (60 shorter events, 15.4 us)
Async XLA Ops:
  6.5 241.6 %copy-start = (bf16[512,1536]{1,0:T(8,128)(2,1)S(1)}, bf16[512,1536]{1,0:T(8,128)(2,1)}, u32[]{:S(2)}) copy-start(bf16[512,1536]{1,0:T(8,128)(2,1)} %param.16) | copy-start | bytes 4718596
  6.5 63.3 %all-gather.4.cloned.1.call-start = ((), (), s32[]{:S(2)}) async-start(), calls=%async_computation.5 | async-start | bytes 3538944 | tf_op jit(solution)/shard_map/all_gather | solution.py:35
  69.9 2.9 copy-start.2
  69.9 3.8 copy-start.7
  75.9 41.7 %all-to-all-start = ((bf16[256,4,1536]{0,2,1:T(8,128)(2,1)}), bf16[256,4,1536]{0,2,1:T(8,128)(2,1)}, u32[]{:S(2)}, u32[]{:S(2)}) async-start(bf16[256,4,1536]{0,2,1:T(8,128)(2,1)} %bitcast.68), calls=%async_computation | async-start | bytes 6291456 | tf_op jit(solution)/shard_map/all_to_all | solution.py:43
  80.6 141.1 %reduce-scatter.3.cloned.1.call-start = ((), (), s32[]{:S(2)}) async-start(), calls=%async_computation.6 | async-start | bytes 11796480 | tf_op jit(solution)/shard_map/reduce_scatter | solution.py:49
  144.9 0.7 copy-start.8
  144.9 0.7 copy-start.9
  144.9 103.2 %all-gather.6.cloned.1.call-start = ((), (), s32[]{:S(2)}) async-start(), calls=%async_computation.7 | async-start | bytes 1310720 | tf_op jit(solution)/shard_map/all_gather | solution.py:72
  222.8 2.5 slice-start
  227.7 2.1 copy-start.3
  231.2 98.4 %all-gather.8.cloned.1.call-start = ((), (), s32[]{:S(2)}) async-start(), calls=%async_computation.8 | async-start | bytes 7864320 | tf_op jit(solution)/shard_map/all_gather | solution.py:77
  252.8 92.3 %all-to-all-start.1 = ((bf16[4,256,1536]{2,1,0:T(8,128)(2,1)}), bf16[4,256,1536]{2,1,0:T(8,128)(2,1)}, u32[]{:S(2)}, u32[]{:S(2)}) async-start(bf16[4,256,1536]{2,1,0:T(8,128)(2,1)} %bitcast.70), calls=%async_computation.2 | async-start | bytes 6291456 | tf_op jit(solution)/shard_map/all_to_all | solution.py:82
  345.2 41.8 %all-to-all-start.2 = ((bf16[4,256,1536]{2,1,0:T(8,128)(2,1)}), bf16[4,256,1536]{2,1,0:T(8,128)(2,1)}, u32[]{:S(2)}, u32[]{:S(2)}) async-start(bf16[4,256,1536]{2,1,0:T(8,128)(2,1)} %bitcast.69), calls=%async_computation.3 | async-start | bytes 6291456 | tf_op jit(solution)/shard_map/all_to_all | solution.py:85
  350.0 174.1 %reduce-scatter.5.cloned.1.call-start = ((), (), s32[]{:S(2)}) async-start(), calls=%async_computation.9 | async-start | bytes 7077888 | tf_op jit(solution)/shard_map/reduce_scatter | solution.py:91
  406.0 119.4 %copy-start.4 = (bf16[1,256,768]{2,1,0:T(8,128)(2,1)S(1)}, bf16[1,256,768]{2,1,0:T(8,128)(2,1)}, u32[]{:S(2)}) copy-start(bf16[1,256,768]{2,1,0:T(8,128)(2,1)} %param.10) | copy-start | bytes 1179652
  406.0 119.4 %copy-start.5 = (s32[1,256,768]{2,1,0:T(8,128)S(1)}, s32[1,256,768]{2,1,0:T(8,128)}, u32[]{:S(2)}) copy-start(s32[1,256,768]{2,1,0:T(8,128)} %param.19) | copy-start | bytes 2359300
  406.0 119.4 %copy-start.6 = (s32[1,256,768]{2,1,0:T(8,128)S(1)}, s32[1,256,768]{2,1,0:T(8,128)}, u32[]{:S(2)}) copy-start(s32[1,256,768]{2,1,0:T(8,128)} %param.18) | copy-start | bytes 2359300
  406.0 120.4 %copy-start.1 = (bf16[512,1536]{1,0:T(8,128)(2,1)S(1)}, bf16[512,1536]{1,0:T(8,128)(2,1)}, u32[]{:S(2)}) copy-start(bf16[512,1536]{1,0:T(8,128)(2,1)} %param.16) | copy-start | bytes 4718596
Sparse Core Ops, SparseCore 0:
  9.5 60.3 all-gather.3
  145.0 76.5 reduce-scatter.2
  231.3 16.8 all-gather.5
  249.6 79.9 all-gather.7
  406.2 117.9 reduce-scatter.4
where the time goes:
time: 536 us; the launch traced here: 533 us
  waiting for transfers between devices  384 us (72%)
  local copies, waits for them, and re-layouts  49.6 us (9%)
  matrix products  44.2 us (8%)
  other arithmetic  27.6 us (5%)
  starting transfers between devices  14.6 us (3%)
  between operations  13.4 us (2%)
    reduce_scatter x1, waiting for transfers between devices, per_device(): lax.psum_scatter(rounded.astype(jnp.float32).astype(jnp.bfloat16), 'gy',...  118 us
    reduce_scatter x1, waiting for transfers between devices, per_device(): lax.psum_scatter(jnp.dot(blocks, joined, preferred_element_type=jnp.float...  76.1 us
    all_gather x1, waiting for transfers between devices, per_device(): lax.all_gather(hidden, 'gx', axis=0, tiled=True)  72 us
    all_gather x1, waiting for transfers between devices, per_device(): whole_rows = lax.all_gather(tokens, 'gy', axis=2, tiled=True)  61.3 us
    all_to_all x1, waiting for transfers between devices, per_device(): lax.all_to_all(feedforward_part.astype(jnp.bfloat16), 'gx', split_axis=0,...  24 us
    all_to_all x1, waiting for transfers between devices, per_device(): lax.all_to_all(normed, 'gx', split_axis=1, concat_axis=0, tiled=True)  23.7 us
    dot_general x1, matrix products, per_device(): jnp.dot(blocks, joined, preferred_element_type=jnp.float32)  22.6 us
    dot_general x1, matrix products, per_device(): jnp.dot(lax.all_gather(hidden, 'gx', axis=0, tiled=True), down_weight, pr...  15.6 us
  transfers between devices with their start and end apart: 8, of which 7 were waited for; matrix products, arithmetic and copies ran while one was open for 10% of the time, Pallas kernels for 0%

commit v1 on v0

v1 whole, which is shorter than its diff:
```python
import jax
import jax.numpy as jnp
from jax import lax
from jax.sharding import PartitionSpec as P

epsilon = 1e-06
keep_scale = 1.0 / 0.9
UP_CHUNKS = 2

f32 = jnp.float32
bf16 = jnp.bfloat16


def layer_norm(values, gain):
    center = values - jnp.mean(values, axis=-1, keepdims=True)
    variance = jnp.mean(center * center, axis=-1, keepdims=True)
    return center * lax.rsqrt(variance + epsilon) * gain


def head_norm(values, gain):
    row_count = values.shape[0]
    shaped = values.reshape(row_count, -1, gain.shape[0])
    return layer_norm(shaped, gain).reshape(row_count, -1)


def mul(left, right):
    return jnp.dot(left, right, preferred_element_type=f32)


def swap(values, bit, n_gx):
    return lax.ppermute(values, "gx", [(i, i ^ bit) for i in range(n_gx)])


def scatter_sum(odd_rows, even_rows, weight, n_gx):
    received = swap(mul(odd_rows, weight).astype(bf16), 1, n_gx)
    total = mul(even_rows, weight).astype(bf16).astype(f32) + received.astype(f32)
    bit, width = 2, weight.shape[1]
    own_rows = 2 * odd_rows.shape[0] // n_gx
    while bit < n_gx:
        pairs = total.reshape(-1, 2, own_rows, width)
        received = swap(pairs[:, 1].astype(bf16), bit, n_gx)
        total = pairs[:, 0] + received.astype(f32)
        bit *= 2
    return total.reshape(own_rows, width)


def gather_pair(own, n_gx):
    held, bit = own, n_gx // 2
    while bit > 1:
        held = jnp.concatenate([held, swap(held, bit, n_gx)], axis=0)
        bit //= 2
    return held, swap(held, 1, n_gx)


def gather_order(n_gx):
    order, bit = [0], n_gx // 2
    while bit >= 1:
        order = order + [p ^ bit for p in order]
        bit //= 2
    return order


def ring_place(index, count):
    return jnp.where(index % 2 == 0, index // 2, count - 1 - index // 2)


def ring_gather(own, ring, place):
    n = len(ring)
    ahead = [(ring[r], ring[(r + 1) % n]) for r in range(n)]
    back = [(b, a) for a, b in ahead]
    forward, backward = [own], [own]
    for step in range(n // 2 - 1):
        forward.append(lax.ppermute(forward[-1], "gy", ahead))
        backward.append(lax.ppermute(backward[-1], "gy", back))
    half = own.shape[0] // 2
    far = jnp.concatenate(
        [
            lax.ppermute(forward[-1][:half], "gy", ahead),
            lax.ppermute(backward[-1][half:], "gy", back),
        ],
        axis=0,
    )
    return jnp.stack(forward + [far] + backward[:0:-1])


def ring_scatter(partial, ring, place):
    n = len(ring)
    half = partial.shape[1] // 2
    ahead = [(ring[r], ring[(r + 1) % n]) for r in range(n)]
    back = [(b, a) for a, b in ahead]

    def block(index, start):
        index = lax.rem(index + 2 * n, n)
        return lax.dynamic_slice(
            partial, (index, start, 0), (1, half, partial.shape[2])
        )[0]

    up, down = block(place - 1, 0), block(place + 1, half)
    for step in range(n - 1):
        came_up = lax.ppermute(up, "gy", ahead)
        came_down = lax.ppermute(down, "gy", back)
        up = came_up.astype(f32) + block(place - 2 - step, 0).astype(f32)
        down = came_down.astype(f32) + block(place + 2 + step, half).astype(f32)
        up, down = up.astype(bf16), down.astype(bf16)
    return jnp.concatenate([up, down], axis=0)


def per_device(
    tokens,
    norm_gain,
    qkv_weight,
    up_weight,
    query_gain,
    key_gain,
    out_weight,
    down_weight,
    attention_keep,
    feedforward_keep,
):
    n_gx, n_gy = lax.axis_size("gx"), lax.axis_size("gy")
    sub = n_gy // n_gx
    me = lax.axis_index("gx")
    ring = list(range(0, n_gy, 2)) + list(range(1, n_gy, 2))[::-1]
    place = ring_place(lax.axis_index("gy"), n_gy)
    images, seq_len, slice_width = tokens.shape
    own_rows = images * seq_len
    block_width = qkv_weight.shape[0]
    head_cols = qkv_weight.shape[2]
    head_size = query_gain.shape[0]

    flat = tokens.reshape(own_rows, slice_width)
    turned = lax.ppermute(
        flat,
        ("gx", "gy"),
        [
            (i * n_gy + k * sub + s, k * n_gy + i * sub + s)
            for i in range(n_gx)
            for k in range(n_gx)
            for s in range(sub)
        ],
    )
    gathered = ring_gather(turned, ring, place)

    wide = flat.astype(f32)
    mean = jnp.mean(wide, axis=1)
    squares = jnp.sum((wide - mean[:, None]) ** 2, axis=1)
    count, bit = slice_width, 1
    while bit < n_gy:
        pairs = [(i, i ^ bit) for i in range(n_gy)]
        other = lax.ppermute(jnp.stack([mean, squares]), "gy", pairs)
        squares = squares + other[1] + (0.5 * count) * (mean - other[0]) ** 2
        mean = 0.5 * (mean + other[0])
        count, bit = 2 * count, 2 * bit
    stats = jnp.stack([mean, lax.rsqrt(squares / count + epsilon)])[None]
    bit = 1
    while bit < n_gx:
        stats = jnp.concatenate([stats, swap(stats, bit, n_gx)], axis=0)
        bit *= 2
    gain = lax.dynamic_slice_in_dim(norm_gain, me * block_width, block_width, 0)

    def normed_rows(position):
        image = me ^ position
        rows = jnp.concatenate(
            [
                lax.dynamic_index_in_dim(
                    gathered,
                    lax.rem(place - ring_place(image * sub + s, n_gy) + n_gy, n_gy),
                    0,
                    keepdims=False,
                )
                for s in range(sub)
            ],
            axis=1,
        ).astype(f32)
        row_mean, row_scale = stats[position, 0], stats[position, 1]
        return ((rows - row_mean[:, None]) * row_scale[:, None] * gain).astype(bf16)

    odd_rows = jnp.concatenate([normed_rows(p) for p in range(1, n_gx, 2)], axis=0)
    even_rows = jnp.concatenate([normed_rows(p) for p in range(0, n_gx, 2)], axis=0)

    qkv_flat = qkv_weight.reshape(block_width, 3 * head_cols)
    united = scatter_sum(odd_rows, even_rows, qkv_flat, n_gx)
    up_cols = up_weight.shape[1] // UP_CHUNKS
    hidden = []
    for c in range(UP_CHUNKS):
        total = scatter_sum(
            odd_rows, even_rows, up_weight[:, c * up_cols : (c + 1) * up_cols], n_gx
        )
        hidden.append(jax.nn.gelu(total, approximate=False).astype(bf16))

    queries = head_norm(united[:, :head_cols], query_gain).astype(bf16)
    keys = head_norm(united[:, head_cols : 2 * head_cols], key_gain).astype(bf16)
    values = united[:, 2 * head_cols :].astype(bf16)
    query_grid = queries.reshape(images, seq_len, -1, head_size)
    key_grid = keys.reshape(images, seq_len, -1, head_size)
    value_grid = values.reshape(images, seq_len, -1, head_size)
    scores = jnp.einsum(
        "bshd,bthd->bhst", query_grid, key_grid, preferred_element_type=f32
    ) * head_size ** (-0.5)
    raised = jnp.exp(scores)
    weights = (raised / jnp.sum(raised, axis=-1, keepdims=True)).astype(bf16)
    attended = jnp.einsum("bhst,bthd->bshd", weights, value_grid, preferred_element_type=f32)
    attended = attended.astype(bf16).reshape(own_rows, head_cols)

    order = gather_order(n_gx)
    def home(devices):
        return [
            (
                k * n_gy + devices[s * n_gx + q],
                (k ^ order[q]) * n_gy + k * sub + s,
            )
            for k in range(n_gx)
            for s in range(sub)
            for q in range(n_gx)
        ]

    def columns(weight, s):
        return weight[:, s * slice_width : (s + 1) * slice_width]

    attended_halves = gather_pair(attended, n_gx)
    attention_out = lax.psum_scatter(
        jnp.concatenate(
            [
                mul(rows, columns(out_weight, s)).astype(bf16)
                for s in range(sub)
                for rows in attended_halves
            ],
            axis=0,
        ),
        "gy",
        scatter_dimension=0,
        tiled=True,
    )
    attention_out = lax.ppermute(attention_out, ("gx", "gy"), home(range(n_gy))).astype(f32)
    hidden_halves = [gather_pair(part, n_gx) for part in hidden]
    pieces = []
    for s in range(sub):
        for half in range(2):
            total = 0.0
            for c in range(UP_CHUNKS):
                weight = down_weight[c * up_cols : (c + 1) * up_cols]
                total = total + mul(hidden_halves[c][half], columns(weight, s))
            pieces.append(total.astype(bf16))
    partial = jnp.concatenate(pieces, axis=0).reshape(n_gy, own_rows, slice_width)
    feedforward_out = ring_scatter(partial, ring, place)
    feedforward_out = lax.ppermute(feedforward_out, ("gx", "gy"), home(ring)).astype(f32)

    shape = tokens.shape
    branches = attention_keep.astype(f32) * attention_out.reshape(
        shape
    ) + feedforward_keep.astype(f32) * feedforward_out.reshape(shape)
    return (tokens.astype(f32) + branches * keep_scale).astype(bf16)


def solution(mesh):
    in_specs = (
        P("gx", None, "gy"),
        P(),
        P("gx", None, "gy"),
        P("gx", "gy"),
        P(),
        P(),
        P("gy", "gx"),
        P("gy", "gx"),
        P("gx", None, "gy"),
        P("gx", None, "gy"),
    )
    out_specs = P("gx", None, "gy")
    return jax.shard_map(
        per_device, mesh=mesh, in_specs=in_specs, out_specs=out_specs, check_vma=False
    )
```

time: 536 us -> 320 us (0.60)
  waiting for transfers between devices: 384 us -> 174 us
  local copies, waits for them, and re-layouts: 49.6 us -> 14 us
  starting transfers between devices: 14.6 us -> 42.1 us
    reduce_scatter x2 -> x1, waiting for transfers between devices: 194 us -> 0.02 us  [per_device(): lax.psum_scatter(jnp.concatenate([mul(rows, columns(out_weight, s)).astyp...]
    ppermute x0 -> x42, waiting for transfers between devices: none -> 174 us  [the longest x14 63.4 us: swap(): return lax.ppermute(values, 'gx', [(i, i ^ bit) for i in range(n_gx)])]
    all_gather x3 -> x0, waiting for transfers between devices: 142 us -> none  [the longest x1 72 us: per_device(): lax.all_gather(hidden, 'gx', axis=0, tiled=True)]
    all_to_all x3 -> x0, waiting for transfers between devices: 47.6 us -> none  [the longest x1 24 us: per_device(): lax.all_to_all(feedforward_part.astype(jnp.bfloat16), 'gx', split_axis=0,...]
    ppermute x0 -> x42, starting transfers between devices: none -> 42.1 us  [the longest x7 7.89 us: ring_scatter(): came_up = lax.ppermute(up, 'gy', ahead)]
    all_to_all x3 -> x0, local copies, waits for them, and re-layouts: 16.7 us -> none  [the longest x1 6 us: per_device(): lax.all_to_all(attention_part.astype(jnp.bfloat16), 'gx', split_axis=0, c...]
    all_to_all x3 -> x0, starting transfers between devices: 14.3 us -> none  [the longest x1 4.86 us: per_device(): lax.all_to_all(feedforward_part.astype(jnp.bfloat16), 'gx', split_axis=0,...]
    another operation x3 -> x1, local copies, waits for them, and re-layouts: 14 us -> 0.03 us  [ring_gather(): return jnp.stack(forward + [far] + backward[:0:-1])]
  transfers between devices with their start and end apart: 8 -> 43, of which waited for: 7 -> 27; matrix products, arithmetic and copies ran while one was open for 10% -> 25% of each run, Pallas kernels for 0% -> 0%
where the time goes in v1:
time: 320 us; the launch traced here: 319 us
  waiting for transfers between devices  174 us (54%)
  matrix products  49.5 us (15%)
  starting transfers between devices  42.1 us (13%)
  other arithmetic  25 us (8%)
  between operations  14.4 us (4%)
  local copies, waits for them, and re-layouts  14 us (4%)
    ppermute x14, waiting for transfers between devices, swap(): return lax.ppermute(values, 'gx', [(i, i ^ bit) for i in range(n_gx)])  63.4 us
    dot_general x18, matrix products, mul(): return jnp.dot(left, right, preferred_element_type=f32)  48.8 us
    ppermute x7, waiting for transfers between devices, ring_scatter(): came_up = lax.ppermute(up, 'gy', ahead)  34 us
    ppermute x3, waiting for transfers between devices, ring_gather(): forward.append(lax.ppermute(forward[-1], 'gy', ahead))  24.3 us
    ppermute x1, waiting for transfers between devices, per_device(): lax.ppermute(attention_out, ('gx', 'gy'), home(range(n_gy))).astype(f32)  22.3 us
    ppermute x1, waiting for transfers between devices, per_device(): lax.ppermute(feedforward_out, ('gx', 'gy'), home(ring)).astype(f32)  10.9 us
    unnamed x51, local copies, waits for them, and re-layouts  10.6 us
    ppermute x7, waiting for transfers between devices, ring_scatter(): came_down = lax.ppermute(down, 'gy', back)  10.2 us
  transfers between devices with their start and end apart: 43, of which 27 were waited for; matrix products, arithmetic and copies ran while one was open for 25% of the time, Pallas kernels for 0%

profile of v1, /device:TPU:2, one launch (start us, length us, event | category | flops | bytes accessed | tf_op | source)
XLA Modules:
  0.0 319.2 jit_solution(9035723459280658667)
XLA Ops:
  17.9 5.2 %collective-permute-start.11 = (f32[2,256]{1,0:T(2,128)S(1)}, f32[2,256]{1,0:T(2,128)S(1)}, u32[]{:S(2)}, u32[]{:S(2)}) collective-permute-start(f32[2,256]{1,0:T(2,128)S(1)} %pad_maximum_fusion.17), channel_id=1, source_target_pairs={{0,4},{1,5},{2,6},{3,7},{4,0},{5,1},{6,2},{7,3},{8,12},{9,13},{10,... | collective-permute-start | bytes 6152 | tf_op jit(solution)/shard_map/ppermute | solution.py:150
  23.1 6.6 %copy.13 = bf16[1536,3,512]{0,2,1:T(8,128)(2,1)} copy(bf16[1536,3,512]{2,0,1:T(8,128)(2,1)} %param.12) | data formatting | bytes 9437184 | tf_op args[2]
  34.1 8.1 %collective-permute-done.1 = bf16[256,768]{1,0:T(8,128)(2,1)S(1)} collective-permute-done((bf16[256,768]{1,0:T(8,128)(2,1)S(1)}, bf16[256,768]{1,0:T(8,128)(2,1)S(1)}, u32[]{:S(2)}, u32[]{:S(2)}) %collective-permute-start.1) | collective-permute-done | bytes 393248 | tf_op jit(solution)/shard_map/ppermute | solution.py:73
  44.2 8.5 %collective-permute-done.2 = bf16[256,768]{1,0:T(8,128)(2,1)S(1)} collective-permute-done((bf16[256,768]{1,0:T(8,128)(2,1)S(1)}, bf16[256,768]{1,0:T(8,128)(2,1)S(1)}, u32[]{:S(2)}, u32[]{:S(2)}) %collective-permute-start.2) | collective-permute-done | bytes 393248 | tf_op jit(solution)/shard_map/ppermute | solution.py:73
  54.9 7.7 %collective-permute-done.3 = bf16[256,768]{1,0:T(8,128)(2,1)S(1)} collective-permute-done((bf16[256,768]{1,0:T(8,128)(2,1)S(1)}, bf16[256,768]{1,0:T(8,128)(2,1)S(1)}, u32[]{:S(2)}, u32[]{:S(2)}) %collective-permute-start.3) | collective-permute-done | bytes 393248 | tf_op jit(solution)/shard_map/ppermute | solution.py:73
  71.4 3.8 %convolution_convert_fusion = bf16[512,1536]{1,0:T(8,128)(2,1)} fusion(bf16[1536,1536]{0,1:T(8,128)(2,1)S(1)} %bitcast.325, bf16[256,1536]{1,0:T(8,128)(2,1)S(1)} %get-tuple-element.38, bf16[256,1536]{1,0:T(8,128)(2,1)S(1)} %get-tuple-element.37), kind=kOutput, calls=%fused_computation.17 | convolution fusion | flops 2419851264 | bytes 7864320 | tf_op jit(solution)/shard_map/dot_general | solution.py:27
  75.2 6.5 %fusion.17 = bf16[512,1536]{1,0:T(8,128)(2,1)} fusion(bf16[1536,3072]{1,0:T(8,128)(2,1)} %param.13, bf16[256,1536]{1,0:T(8,128)(2,1)S(1)} %get-tuple-element.38, bf16[256,1536]{1,0:T(8,128)(2,1)S(1)} %get-tuple-element.37), kind=kOutput, calls=%fused_computation.16 | convolution fusion | flops 2419851264 | bytes 7864320 | tf_op jit(solution)/shard_map/dot_general | solution.py:27
  82.3 6.4 %fusion.11 = bf16[512,1536]{1,0:T(8,128)(2,1)} fusion(bf16[1536,3072]{1,0:T(8,128)(2,1)} %param.13, bf16[256,1536]{1,0:T(8,128)(2,1)S(1)} %get-tuple-element.38, bf16[256,1536]{1,0:T(8,128)(2,1)S(1)} %get-tuple-element.37), kind=kOutput, calls=%fused_computation.14 | convolution fusion | flops 2419851264 | bytes 7864320 | tf_op jit(solution)/shard_map/dot_general | solution.py:27
  88.8 4.0 %convert_add_fusion.2 = f32[512,1536]{1,0:T(8,128)S(1)} fusion(bf16[512,1536]{1,0:T(8,128)(2,1)} %collective-permute-done.14, bf16[1536,1536]{0,1:T(8,128)(2,1)S(1)} %bitcast.328, bf16[256,1536]{1,0:T(8,128)(2,1)S(1)} %get-tuple-element.36, bf16[256,1536]{1,0:T(8,128)(2,1)S(1)} %get-tuple-element.35), kind=kOutput, calls=%fused_computation.12 | convolution fusion | flops 2422210560 | bytes 11010048 | tf_op jit(solution)/shard_map/dot_general | solution.py:27
  96.9 5.4 %convert_add_fusion = f32[512,1536]{1,0:T(8,128)S(1)} fusion(bf16[512,1536]{1,0:T(8,128)(2,1)} %collective-permute-done.22, bf16[1536,3072]{1,0:T(8,128)(2,1)} %param.13, bf16[256,1536]{1,0:T(8,128)(2,1)S(1)} %copy-done.8, bf16[256,1536]{1,0:T(8,128)(2,1)S(1)} %copy-done.6), kind=kOutput, calls=%fused_computation.10 | convolution fusion | flops 2422210560 | bytes 11010048 | tf_op jit(solution)/shard_map/dot_general | solution.py:27
  105.5 5.4 %convert_add_fusion.1 = f32[512,1536]{1,0:T(8,128)S(1)} fusion(bf16[512,1536]{1,0:T(8,128)(2,1)} %collective-permute-done.19, bf16[1536,3072]{1,0:T(8,128)(2,1)} %param.13, bf16[256,1536]{1,0:T(8,128)(2,1)S(1)} %copy-done.8, bf16[256,1536]{1,0:T(8,128)(2,1)S(1)} %copy-done.6), kind=kOutput, calls=%fused_computation.11 | convolution fusion | flops 2422210560 | bytes 11010048 | tf_op jit(solution)/shard_map/dot_general | solution.py:27
  111.3 6.2 %collective-permute-done.15 = bf16[1,256,1536]{1,2,0:T(8,128)(2,1)S(1)} collective-permute-done((bf16[1,256,1536]{1,2,0:T(8,128)(2,1)}, bf16[1,256,1536]{1,2,0:T(8,128)(2,1)S(1)}, u32[]{:S(2)}, u32[]{:S(2)}) %collective-permute-start.15) | collective-permute-done | bytes 786464 | tf_op jit(solution)/shard_map/ppermute | solution.py:31
  119.0 15.5 %collective-permute-done.23 = bf16[1,256,1536]{2,1,0:T(8,128)(2,1)} collective-permute-done((bf16[1,256,1536]{2,1,0:T(8,128)(2,1)}, bf16[1,256,1536]{2,1,0:T(8,128)(2,1)}, u32[]{:S(2)}, u32[]{:S(2)}) %collective-permute-start.23) | collective-permute-done | bytes 786464 | tf_op jit(solution)/shard_map/ppermute | solution.py:31
  134.5 4.8 %fusion.45 = bf16[256,1536]{1,0:T(8,128)(2,1)S(1)} fusion(bf16[1,256,1536]{2,1,0:T(8,128)(2,1)} %collective-permute-done.23, f32[1,2,256,1536]{3,2,1,0:T(8,128)} %bitcast.331), kind=kLoop, calls=%fused_computation.42 | loop fusion | flops 26345472 | bytes 3145728 | tf_op jit(solution)/shard_map/convert_element_type | solution.py:189
  139.4 12.0 %collective-permute-done.20 = bf16[1,256,1536]{2,1,0:T(8,128)(2,1)} collective-permute-done((bf16[1,256,1536]{2,1,0:T(8,128)(2,1)S(1)}, bf16[1,256,1536]{2,1,0:T(8,128)(2,1)}, u32[]{:S(2)}, u32[]{:S(2)}) %collective-permute-start.20) | collective-permute-done | bytes 786464 | tf_op jit(solution)/shard_map/ppermute | solution.py:31
  151.4 4.5 %fusion.42 = bf16[256,1536]{1,0:T(8,128)(2,1)S(1)} fusion(bf16[1,256,1536]{2,1,0:T(8,128)(2,1)} %collective-permute-done.20, f32[1,2,256,1536]{3,2,1,0:T(8,128)S(1)} %bitcast.333), kind=kLoop, calls=%fused_computation.39 | loop fusion | flops 26345472 | bytes 3145728 | tf_op jit(solution)/shard_map/convert_element_type | solution.py:189
  162.0 28.1 %collective-permute-done.21 = bf16[256,1536]{1,0:T(8,128)(2,1)S(1)} collective-permute-done((bf16[256,1536]{1,0:T(8,128)(2,1)S(1)}, bf16[256,1536]{1,0:T(8,128)(2,1)S(1)}, u32[]{:S(2)}, u32[]{:S(2)}) %collective-permute-start.21) | collective-permute-done | bytes 786464 | tf_op jit(solution)/shard_map/ppermute | solution.py:31
  208.3 4.9 %collective-permute-done.27 = bf16[128,768]{1,0:T(8,128)(2,1)} collective-permute-done((bf16[128,768]{1,0:T(8,128)(2,1)S(1)}, bf16[128,768]{1,0:T(8,128)(2,1)}, u32[]{:S(2)}, u32[]{:S(2)}) %collective-permute-start.27) | collective-permute-done | bytes 196640 | tf_op jit(solution)/shard_map/ppermute | solution.py:100
  217.5 4.0 %collective-permute-done.28 = bf16[128,768]{1,0:T(8,128)(2,1)S(1)} collective-permute-done((bf16[128,768]{1,0:T(8,128)(2,1)S(1)}, bf16[128,768]{1,0:T(8,128)(2,1)S(1)}, u32[]{:S(2)}, u32[]{:S(2)}) %collective-permute-start.28) | collective-permute-done | bytes 196640 | tf_op jit(solution)/shard_map/ppermute | solution.py:100
  227.9 9.0 %collective-permute-done.29 = bf16[128,768]{1,0:T(8,128)(2,1)S(1)} collective-permute-done((bf16[128,768]{1,0:T(8,128)(2,1)S(1)}, bf16[128,768]{1,0:T(8,128)(2,1)S(1)}, u32[]{:S(2)}, u32[]{:S(2)}) %collective-permute-start.29) | collective-permute-done | bytes 196640 | tf_op jit(solution)/shard_map/ppermute | solution.py:100
  248.8 3.9 %collective-permute-done.31 = bf16[128,768]{1,0:T(8,128)(2,1)S(1)} collective-permute-done((bf16[128,768]{1,0:T(8,128)(2,1)S(1)}, bf16[128,768]{1,0:T(8,128)(2,1)S(1)}, u32[]{:S(2)}, u32[]{:S(2)}) %collective-permute-start.31) | collective-permute-done | bytes 196640 | tf_op jit(solution)/shard_map/ppermute | solution.py:100
  257.7 5.2 %collective-permute-done.32 = bf16[128,768]{1,0:T(8,128)(2,1)S(1)} collective-permute-done((bf16[128,768]{1,0:T(8,128)(2,1)S(1)}, bf16[128,768]{1,0:T(8,128)(2,1)S(1)}, u32[]{:S(2)}, u32[]{:S(2)}) %collective-permute-start.32) | collective-permute-done | bytes 196640 | tf_op jit(solution)/shard_map/ppermute | solution.py:100
  278.1 10.9 %collective-permute-done.41 = bf16[256,768]{1,0:T(8,128)(2,1)S(1)} collective-permute-done((bf16[256,768]{1,0:T(8,128)(2,1)S(1)}, bf16[256,768]{1,0:T(8,128)(2,1)S(1)}, u32[]{:S(2)}, u32[]{:S(2)}) %collective-permute-start.41) | collective-permute-done | bytes 393248 | tf_op jit(solution)/shard_map/ppermute | solution.py:246
  289.0 22.3 %collective-permute-done.18 = bf16[256,768]{1,0:T(8,128)(2,1)S(1)} collective-permute-done((bf16[256,768]{1,0:T(8,128)(2,1)}, bf16[256,768]{1,0:T(8,128)(2,1)S(1)}, u32[]{:S(2)}, u32[]{:S(2)}) %collective-permute-start.18) | collective-permute-done | bytes 393248 | tf_op jit(solution)/shard_map/ppermute | solution.py:234
  (188 shorter events, 105.8 us)
Async XLA Ops:
  6.5 269.1 %reduce-scatter.2.cloned.1.call-start = ((), (), s32[]{:S(2)}) async-start(), calls=%async_computation.1 | async-start | bytes 3538944 | tf_op jit(solution)/shard_map/reduce_scatter | solution.py:221
  6.5 24.1 %collective-permute-start = (bf16[256,768]{1,0:T(8,128)(2,1)}, bf16[256,768]{1,0:T(8,128)(2,1)S(1)}, u32[]{:S(2)}, u32[]{:S(2)}) collective-permute-start(bf16[256,768]{1,0:T(8,128)(2,1)} %bitcast.329), channel_id=1, source_target_pairs={{0,0},{1,1},{2,8},{3,9},{4,16},{5,17},{6,24},{7,25},{8,2},{9,3},{1... | collective-permute-start | bytes 1179656 | tf_op jit(solution)/shard_map/ppermute | solution.py:132
  17.9 12.6 %collective-permute-start.11 = (f32[2,256]{1,0:T(2,128)S(1)}, f32[2,256]{1,0:T(2,128)S(1)}, u32[]{:S(2)}, u32[]{:S(2)}) collective-permute-start(f32[2,256]{1,0:T(2,128)S(1)} %pad_maximum_fusion.17), channel_id=1, source_target_pairs={{0,4},{1,5},{2,6},{3,7},{4,0},{5,1},{6,2},{7,3},{8,12},{9,13},{10,... | collective-permute-start | bytes 6152 | tf_op jit(solution)/shard_map/ppermute | solution.py:150
  30.6 11.5 %collective-permute-start.1 = (bf16[256,768]{1,0:T(8,128)(2,1)S(1)}, bf16[256,768]{1,0:T(8,128)(2,1)S(1)}, u32[]{:S(2)}, u32[]{:S(2)}) collective-permute-start(bf16[256,768]{1,0:T(8,128)(2,1)S(1)} %collective-permute-done), channel_id=1, source_target_pairs={{0,2},{2,4},{4,6},{6,7},{7,5},{5,3},{3,1},{1,0},{8,10},{10,12},{12... | collective-permute-start | bytes 1179656 | tf_op jit(solution)/shard_map/ppermute | solution.py:73
  31.2 11.5 %collective-permute-start.5 = (bf16[256,768]{1,0:T(8,128)(2,1)S(1)}, bf16[256,768]{1,0:T(8,128)(2,1)S(1)}, u32[]{:S(2)}, u32[]{:S(2)}) collective-permute-start(bf16[256,768]{1,0:T(8,128)(2,1)S(1)} %collective-permute-done), channel_id=1, source_target_pairs={{2,0},{4,2},{6,4},{7,6},{5,7},{3,5},{1,3},{0,1},{10,8},{12,10},{14... | collective-permute-start | bytes 1179656 | tf_op jit(solution)/shard_map/ppermute | solution.py:74
  32.7 11.5 %collective-permute-start.13 = (f32[2,2,256]{2,1,0:T(2,128)S(1)}, f32[2,2,256]{2,1,0:T(2,128)S(1)}, u32[]{:S(2)}, u32[]{:S(2)}) collective-permute-start(f32[2,2,256]{2,1,0:T(2,128)S(1)} %pad_maximum_fusion.14), channel_id=1, source_target_pairs={{0,16},{8,24},{16,0},{24,8},{1,17},{9,25},{17,1},{25,9},{2,18},{10... | collective-permute-start | bytes 12296 | tf_op jit(solution)/shard_map/ppermute | solution.py:31
  42.2 10.6 %collective-permute-start.2 = (bf16[256,768]{1,0:T(8,128)(2,1)S(1)}, bf16[256,768]{1,0:T(8,128)(2,1)S(1)}, u32[]{:S(2)}, u32[]{:S(2)}) collective-permute-start(bf16[256,768]{1,0:T(8,128)(2,1)S(1)} %collective-permute-done.1), channel_id=1, source_target_pairs={{0,2},{2,4},{4,6},{6,7},{7,5},{5,3},{3,1},{1,0},{8,10},{10,12},{12... | collective-permute-start | bytes 1179656 | tf_op jit(solution)/shard_map/ppermute | solution.py:73
  42.7 10.6 %collective-permute-start.6 = (bf16[256,768]{1,0:T(8,128)(2,1)S(1)}, bf16[256,768]{1,0:T(8,128)(2,1)S(1)}, u32[]{:S(2)}, u32[]{:S(2)}) collective-permute-start(bf16[256,768]{1,0:T(8,128)(2,1)S(1)} %collective-permute-done.5), channel_id=1, source_target_pairs={{2,0},{4,2},{6,4},{7,6},{5,7},{3,5},{1,3},{0,1},{10,8},{12,10},{14... | collective-permute-start | bytes 1179656 | tf_op jit(solution)/shard_map/ppermute | solution.py:74
  53.3 9.8 %collective-permute-start.7 = (bf16[256,768]{1,0:T(8,128)(2,1)S(1)}, bf16[256,768]{1,0:T(8,128)(2,1)S(1)}, u32[]{:S(2)}, u32[]{:S(2)}) collective-permute-start(bf16[256,768]{1,0:T(8,128)(2,1)S(1)} %collective-permute-done.6), channel_id=1, source_target_pairs={{2,0},{4,2},{6,4},{7,6},{5,7},{3,5},{1,3},{0,1},{10,8},{12,10},{14... | collective-permute-start | bytes 1179656 | tf_op jit(solution)/shard_map/ppermute | solution.py:74
  75.2 13.6 %collective-permute-start.14 = (bf16[512,1536]{1,0:T(8,128)(2,1)}, bf16[512,1536]{1,0:T(8,128)(2,1)}, u32[]{:S(2)}, u32[]{:S(2)}) collective-permute-start(bf16[512,1536]{1,0:T(8,128)(2,1)} %convolution_convert_fusion), channel_id=1, source_target_pairs={{0,8},{8,0},{16,24},{24,16},{1,9},{9,1},{17,25},{25,17},{2,10},{10... | collective-permute-start | bytes 4718600 | tf_op jit(solution)/shard_map/ppermute | solution.py:31
  81.8 15.1 %collective-permute-start.22 = (bf16[512,1536]{1,0:T(8,128)(2,1)}, bf16[512,1536]{1,0:T(8,128)(2,1)}, u32[]{:S(2)}, u32[]{:S(2)}) collective-permute-start(bf16[512,1536]{1,0:T(8,128)(2,1)} %fusion.17), channel_id=1, source_target_pairs={{0,8},{8,0},{16,24},{24,16},{1,9},{9,1},{17,25},{25,17},{2,10},{10... | collective-permute-start | bytes 4718600 | tf_op jit(solution)/shard_map/ppermute | solution.py:31
  88.7 16.7 %collective-permute-start.19 = (bf16[512,1536]{1,0:T(8,128)(2,1)}, bf16[512,1536]{1,0:T(8,128)(2,1)}, u32[]{:S(2)}, u32[]{:S(2)}) collective-permute-start(bf16[512,1536]{1,0:T(8,128)(2,1)} %fusion.11), channel_id=1, source_target_pairs={{0,8},{8,0},{16,24},{24,16},{1,9},{9,1},{17,25},{25,17},{2,10},{10... | collective-permute-start | bytes 4718600 | tf_op jit(solution)/shard_map/ppermute | solution.py:31
  96.9 20.6 %collective-permute-start.15 = (bf16[1,256,1536]{1,2,0:T(8,128)(2,1)}, bf16[1,256,1536]{1,2,0:T(8,128)(2,1)S(1)}, u32[]{:S(2)}, u32[]{:S(2)}) collective-permute-start(bf16[1,256,1536]{1,2,0:T(8,128)(2,1)} %bitcast.338), channel_id=1, source_target_pairs={{0,16},{8,24},{16,0},{24,8},{1,17},{9,25},{17,1},{25,9},{2,18},{10... | collective-permute-start | bytes 2359304 | tf_op jit(solution)/shard_map/ppermute | solution.py:31
  103.4 31.1 %collective-permute-start.23 = (bf16[1,256,1536]{2,1,0:T(8,128)(2,1)}, bf16[1,256,1536]{2,1,0:T(8,128)(2,1)}, u32[]{:S(2)}, u32[]{:S(2)}) collective-permute-start(bf16[1,256,1536]{2,1,0:T(8,128)(2,1)} %fusion.91), channel_id=1, source_target_pairs={{0,16},{8,24},{16,0},{24,8},{1,17},{9,25},{17,1},{25,9},{2,18},{10... | collective-permute-start | bytes 2359304 | tf_op jit(solution)/shard_map/ppermute | solution.py:31
  111.0 40.4 %collective-permute-start.20 = (bf16[1,256,1536]{2,1,0:T(8,128)(2,1)S(1)}, bf16[1,256,1536]{2,1,0:T(8,128)(2,1)}, u32[]{:S(2)}, u32[]{:S(2)}) collective-permute-start(bf16[1,256,1536]{2,1,0:T(8,128)(2,1)S(1)} %fusion.90), channel_id=1, source_target_pairs={{0,16},{8,24},{16,0},{24,8},{1,17},{9,25},{17,1},{25,9},{2,18},{10... | collective-permute-start | bytes 2359304 | tf_op jit(solution)/shard_map/ppermute | solution.py:31
  119.0 37.9 %collective-permute-start.16 = (bf16[256,512]{0,1:T(8,128)(2,1)S(1)}, bf16[256,512]{0,1:T(8,128)(2,1)S(1)}, u32[]{:S(2)}, u32[]{:S(2)}) collective-permute-start(bf16[256,512]{0,1:T(8,128)(2,1)S(1)} %bitcast.340), channel_id=1, source_target_pairs={{0,16},{8,24},{16,0},{24,8},{1,17},{9,25},{17,1},{25,9},{2,18},{10... | collective-permute-start | bytes 786440 | tf_op jit(solution)/shard_map/ppermute | solution.py:31
  139.3 51.0 %collective-permute-start.24 = (bf16[256,1536]{1,0:T(8,128)(2,1)S(1)}, bf16[256,1536]{1,0:T(8,128)(2,1)S(1)}, u32[]{:S(2)}, u32[]{:S(2)}) collective-permute-start(bf16[256,1536]{1,0:T(8,128)(2,1)S(1)} %fusion.45), channel_id=1, source_target_pairs={{0,16},{8,24},{16,0},{24,8},{1,17},{9,25},{17,1},{25,9},{2,18},{10... | collective-permute-start | bytes 2359304 | tf_op jit(solution)/shard_map/ppermute | solution.py:31
  155.9 34.2 %collective-permute-start.21 = (bf16[256,1536]{1,0:T(8,128)(2,1)S(1)}, bf16[256,1536]{1,0:T(8,128)(2,1)S(1)}, u32[]{:S(2)}, u32[]{:S(2)}) collective-permute-start(bf16[256,1536]{1,0:T(8,128)(2,1)S(1)} %fusion.42), channel_id=1, source_target_pairs={{0,16},{8,24},{16,0},{24,8},{1,17},{9,25},{17,1},{25,9},{2,18},{10... | collective-permute-start | bytes 2359304 | tf_op jit(solution)/shard_map/ppermute | solution.py:31
  190.1 12.8 %collective-permute-start.25 = (bf16[512,1536]{1,0:T(8,128)(2,1)S(1)}, bf16[512,1536]{1,0:T(8,128)(2,1)S(1)}, u32[]{:S(2)}, u32[]{:S(2)}) collective-permute-start(bf16[512,1536]{1,0:T(8,128)(2,1)S(1)} %pad_maximum_fusion.4), channel_id=1, source_target_pairs={{0,8},{8,0},{16,24},{24,16},{1,9},{9,1},{17,25},{25,17},{2,10},{10... | collective-permute-start | bytes 4718600 | tf_op jit(solution)/shard_map/ppermute | solution.py:31
  190.4 9.9 %collective-permute-start.26 = (bf16[512,1536]{1,0:T(8,128)(2,1)S(1)}, bf16[512,1536]{1,0:T(8,128)(2,1)S(1)}, u32[]{:S(2)}, u32[]{:S(2)}) collective-permute-start(bf16[512,1536]{1,0:T(8,128)(2,1)S(1)} %pad_maximum_fusion.5), channel_id=1, source_target_pairs={{0,8},{8,0},{16,24},{24,16},{1,9},{9,1},{17,25},{25,17},{2,10},{10... | collective-permute-start | bytes 4718600 | tf_op jit(solution)/shard_map/ppermute | solution.py:31
  225.8 11.1 %collective-permute-start.29 = (bf16[128,768]{1,0:T(8,128)(2,1)S(1)}, bf16[128,768]{1,0:T(8,128)(2,1)S(1)}, u32[]{:S(2)}, u32[]{:S(2)}) collective-permute-start(bf16[128,768]{1,0:T(8,128)(2,1)S(1)} %get-tuple-element.19), channel_id=1, source_target_pairs={{0,2},{2,4},{4,6},{6,7},{7,5},{5,3},{3,1},{1,0},{8,10},{10,12},{12... | collective-permute-start | bytes 589832 | tf_op jit(solution)/shard_map/ppermute | solution.py:100
  225.9 11.0 %collective-permute-start.36 = (bf16[128,768]{1,0:T(8,128)(2,1)S(1)}, bf16[128,768]{1,0:T(8,128)(2,1)S(1)}, u32[]{:S(2)}, u32[]{:S(2)}) collective-permute-start(bf16[128,768]{1,0:T(8,128)(2,1)S(1)} %get-tuple-element.20), channel_id=1, source_target_pairs={{2,0},{4,2},{6,4},{7,6},{5,7},{3,5},{1,3},{0,1},{10,8},{12,10},{14... | collective-permute-start | bytes 589832 | tf_op jit(solution)/shard_map/ppermute | solution.py:101
  273.7 15.3 %collective-permute-start.41 = (bf16[256,768]{1,0:T(8,128)(2,1)S(1)}, bf16[256,768]{1,0:T(8,128)(2,1)S(1)}, u32[]{:S(2)}, u32[]{:S(2)}) collective-permute-start(bf16[256,768]{1,0:T(8,128)(2,1)S(1)} %pad_maximum_fusion.13), channel_id=1, source_target_pairs={{0,0},{2,16},{4,8},{6,24},{7,1},{5,17},{3,9},{1,25},{8,10},{10,26}... | collective-permute-start | bytes 1179656 | tf_op jit(solution)/shard_map/ppermute | solution.py:246
  275.6 35.7 %collective-permute-start.18 = (bf16[256,768]{1,0:T(8,128)(2,1)}, bf16[256,768]{1,0:T(8,128)(2,1)S(1)}, u32[]{:S(2)}, u32[]{:S(2)}) collective-permute-start(bf16[256,768]{1,0:T(8,128)(2,1)} %reduce-scatter.2.cloned.1.call-done), channel_id=1, source_target_pairs={{0,0},{1,16},{2,8},{3,24},{4,1},{5,17},{6,9},{7,25},{8,10},{9,26},... | collective-permute-start | bytes 1179656 | tf_op jit(solution)/shard_map/ppermute | solution.py:234
  (40 other events, 442.0 us)
Sparse Core Ops, SparseCore 0:
  162.1 79.3 reduce-scatter.1
